TPU v7x, 128 devices: a whole 4x4x4 slice. The times are simulated.
128 devices in a mesh: row: 8 (over z, y_lo), col: 16 (over y_hi, x, core).
Axes of the slice: x: 4, y: 4 (y_hi: 2, y_lo: 2; y = y_hi * 2 + y_lo), z: 4, core: 2. Of those that a mesh axis runs over, the one named last changes fastest.
Arguments:
- blocks: float32 [8, 16, 170, 128, 128], P('row', 'col'), may hold values from -1 to 1
- coords: int32 [8, 16, 2, 170], P('row', 'col'), may hold values from 0 to 31, as said below
- vectors: float32 [2, 32768, 128], P(None, ('row', 'col')), may hold values from -6 to 6
Outputs:
- basis: float32 [2, 32768, 128], P(None, ('row', 'col'))
Inputs may be any that keep to these rules, and one draw needn't show every extreme that they name: Within each tile the 170 listed positions are distinct, and the positions (0, 0) and (31, 15) are always listed; coords[r, c, 0, k] is below 32 and coords[r, c, 1, k] below 16.
All inputs are finite; a program needn't handle non-finite values.
Results may differ from a plain program's by a relative error of at most 0.0003.
Values sent between devices are 32-bit elements; how exact they have to be, the bound alone decides.
A program may use at most 192 MiB of HBM per device.

v0:
```python
import jax
import jax.numpy as jnp
from jax import lax
from jax.sharding import PartitionSpec as P

APPS = 2
exact_mode = lax.Precision.HIGHEST


def tile_products(values, places, col_side, row_side):
    blk_size = values.shape[1]
    listed = values.shape[0]
    row_blocks = row_side.shape[0] // blk_size
    col_blocks = col_side.shape[0] // blk_size
    row_of = places[0]
    col_of = places[1]
    col_pieces = col_side.reshape(col_blocks, blk_size, -1)[col_of]
    direct = jnp.einsum("kab,kbv->kav", values, col_pieces, precision=exact_mode)
    row_pieces = row_side.reshape(row_blocks, blk_size, -1)[row_of]
    flipped = jnp.einsum("kba,kbv->kav", values, row_pieces, precision=exact_mode)
    row_hot = (row_of[None, :] == jnp.arange(row_blocks, dtype=jnp.int32)[:, None]).astype(
        values.dtype
    )
    col_hot = (col_of[None, :] == jnp.arange(col_blocks, dtype=jnp.int32)[:, None]).astype(
        values.dtype
    )
    out_rows = jnp.dot(row_hot, direct.reshape(listed, -1), precision=exact_mode).reshape(
        row_side.shape[0], -1
    )
    out_cols = jnp.dot(col_hot, flipped.reshape(listed, -1), precision=exact_mode).reshape(
        col_side.shape[0], -1
    )
    return (out_rows, out_cols)


def normal_basis(applied, factor):
    return lax.linalg.triangular_solve(
        factor, applied, left_side=False, lower=True, transpose_a=True
    )


def local(blocks, coords, vectors):
    n_rowdev = lax.axis_size("row")
    n_coldev = lax.axis_size("col")
    group_rows = vectors.shape[1]
    total_rows = 2 * group_rows * n_rowdev * n_coldev
    values = blocks.reshape(blocks.shape[2], blocks.shape[3], blocks.shape[4])
    places = coords.reshape(2, coords.shape[3])
    start = (vectors[0], vectors[1])
    current = start
    for app_index in range(APPS):
        col_side = lax.all_gather(current[1], "row", axis=0, tiled=True)
        row_side = lax.all_gather(current[0], "col", axis=0, tiled=True)
        out_rows, out_cols = tile_products(values, places, col_side, row_side)
        new_upper = lax.psum_scatter(out_rows, "col", scatter_dimension=0, tiled=True)
        new_lower = lax.psum_scatter(out_cols, "row", scatter_dimension=0, tiled=True)
        applied = (new_upper, new_lower)
        factor_upper, factor_lower = applied
        partial_gram = jnp.einsum("nv,nw->vw", factor_upper, factor_upper, precision=exact_mode)
        partial_gram = partial_gram + jnp.einsum(
            "nv,nw->vw", factor_lower, factor_lower, precision=exact_mode
        )
        gram_sum = lax.psum(partial_gram, ("row", "col")) / total_rows
        factor = jnp.linalg.cholesky(gram_sum)
        current = (normal_basis(applied[0], factor), normal_basis(applied[1], factor))
    upper, lower = current
    return jnp.stack([upper, lower])


def solution(mesh):
    return jax.shard_map(
        local,
        mesh=mesh,
        in_specs=(
            P("row", "col", None, None, None),
            P("row", "col", None, None),
            P(None, ("row", "col"), None),
        ),
        out_specs=P(None, ("row", "col"), None),
        check_vma=False,
    )
```

profile of v0, /device:TPU:1, one launch (start us, length us, event | category | flops | bytes accessed | tf_op | source)
XLA Modules:
  0.0 845.6 jit_solution(6474394078749091209)
XLA Ops:
  6.5 1.7 fusion.38
  10.6 37.6 %all-gather.11.cloned.1.call-done = f32[1,2048,128]{2,1,0:T(8,128)} async-done(((f32[1,256,128]{2,1,0:T(8,128)}), f32[1,2048,128]{2,1,0:T(8,128)}) %all-gather.11.cloned.1.call-update) | async-done | bytes 1048592 | tf_op jit(solution)/shard_map/all_gather | solution.py:52
  48.2 11.6 %gather_fusion = f32[170,128,128]{2,1,0:T(8,128)} fusion(f32[16,128,128]{2,1,0:T(8,128)} %bitcast.108, s32[1024]{0:T(1024)S(1)} %pad_clamp_fusion.1), kind=kCustom, calls=%fused_computation | custom fusion | bytes 22282920 | tf_op jit(solution)/shard_map/gather | solution.py:17
  59.8 23.3 %fusion.8 = f32[170,128,128]{1,2,0:T(8,128)} fusion(f32[170,128,128]{2,1,0:T(8,128)} %gather_fusion, f32[1,1,170,128,128]{4,3,2,1,0:T(8,128)} %param.6), kind=kOutput, calls=%fused_computation.12 | convolution fusion | flops 4278190080 | bytes 33423360 | tf_op jit(solution)/shard_map/kab,kbv->kav/dot_general | solution.py:18
  83.1 12.3 %copy.12 = f32[170,128,128]{2,1,0:T(8,128)} copy(f32[170,128,128]{1,2,0:T(8,128)} %fusion.8) | data formatting | bytes 22282240 | tf_op jit(solution)/shard_map/kab,kbv->kav/dot_general | solution.py:18
  95.3 10.5 %pad.6 = f32[176,128,128]{2,1,0:T(8,128)} pad(f32[170,128,128]{2,1,0:T(8,128)} %copy.12, f32[]{:T(128)} %constant.31.clone.2), padding=0_6x0_0x0_0 | pad | bytes 22675460
  105.8 18.3 %copy.38 = f32[22,8,128,128]{3,1,2,0:T(8,128)} copy(f32[22,8,128,128]{3,2,1,0:T(8,128)} %bitcast.115) | data formatting | bytes 23068672
  124.1 7.0 fusion.31
  131.2 1.5 reshape.116
  132.8 12.0 %gather_fusion.1 = f32[170,128,128]{2,1,0:T(8,128)} fusion(f32[32,128,128]{2,1,0:T(8,128)} %bitcast.110, s32[1024]{0:T(1024)S(1)} %pad_clamp_fusion), kind=kCustom, calls=%fused_computation.1 | custom fusion | bytes 22282920 | tf_op jit(solution)/shard_map/gather | solution.py:19
  144.8 23.4 %fusion.11 = f32[170,128,128]{1,2,0:T(8,128)} fusion(f32[170,128,128]{2,1,0:T(8,128)} %gather_fusion.1, f32[1,1,170,128,128]{4,3,2,1,0:T(8,128)} %param.6), kind=kOutput, calls=%fused_computation.13 | convolution fusion | flops 4278190080 | bytes 33423360 | tf_op jit(solution)/shard_map/kba,kbv->kav/dot_general | solution.py:20
  168.2 12.0 %copy.14 = f32[170,128,128]{2,1,0:T(8,128)} copy(f32[170,128,128]{1,2,0:T(8,128)} %fusion.11) | data formatting | bytes 22282240 | tf_op jit(solution)/shard_map/kba,kbv->kav/dot_general | solution.py:20
  180.3 10.4 %pad.7 = f32[176,128,128]{2,1,0:T(8,128)} pad(f32[170,128,128]{2,1,0:T(8,128)} %copy.14, f32[]{:T(128)} %constant.31.clone.2), padding=0_6x0_0x0_0 | pad | bytes 22675460
  190.7 18.4 %copy.39 = f32[22,8,128,128]{3,1,2,0:T(8,128)} copy(f32[22,8,128,128]{3,2,1,0:T(8,128)} %bitcast.117) | data formatting | bytes 23068672
  209.1 7.0 fusion.33
  216.1 1.1 reshape.119
  217.3 1.4 fusion.40
  218.7 39.3 %reduce-scatter.7.cloned.1.call-done = f32[256,128]{1,0:T(8,128)} async-done(((f32[2048,128]{1,0:T(8,128)}), f32[256,128]{1,0:T(8,128)}) %reduce-scatter.7.cloned.1.call-update) | async-done | bytes 131088 | tf_op jit(solution)/shard_map/reduce_scatter | solution.py:56
  258.0 2.0 convolution_add_fusion.1
  260.0 144.0 %all-reduce.3.cloned.1.call-done = f32[128,128]{0,1:T(8,128)} async-done(((f32[128,128]{0,1:T(8,128)}), f32[128,128]{0,1:T(8,128)}) %all-reduce.3.cloned.1.call-update) | async-done | bytes 65552 | tf_op jit(solution)/shard_map/psum | solution.py:63
  405.8 11.7 %cholesky.44 = f32[128,128]{1,0:T(8,128)S(1)} custom-call(f32[128,128]{1,0:T(8,128)S(1)} %fusion.27), custom_call_target="Cholesky" | custom-call | tf_op jit(solution)/shard_map/jit(cholesky)/cholesky | solution.py:64
  418.9 9.8 %custom-call.8 = f32[1,128,128]{1,2,0:T(8,128)S(1)} custom-call(f32[1,128,128]{2,1,0:T(8,128)S(1)} %fusion.20), custom_call_target="InvertDiagBlocksLowerTriangular" | custom-call | tf_op jit(solution)/shard_map/triangular_solve/custom-call.0 | solution.py:37
  428.7 1.9 convolution_bitcast_fusion.3
  430.6 1.9 convolution_bitcast_fusion.2
  432.6 31.0 %all-gather.7.cloned.1.call-done = f32[2048,128]{0,1:T(8,128)} async-done(((f32[256,128]{0,1:T(8,128)}), f32[2048,128]{0,1:T(8,128)}) %all-gather.7.cloned.1.call-update) | async-done | bytes 1048592 | tf_op jit(solution)/shard_map/all_gather | solution.py:52
  463.6 1.5 copy.36
  465.1 5.3 gather_fusion.2
  470.5 23.5 %fusion.14 = f32[170,128,128]{1,2,0:T(8,128)} fusion(f32[170,128,128]{2,1,0:T(8,128)} %gather_fusion.2, f32[1,1,170,128,128]{4,3,2,1,0:T(8,128)} %param.6), kind=kOutput, calls=%fused_computation.14 | convolution fusion | flops 4278190080 | bytes 33423360 | tf_op jit(solution)/shard_map/kab,kbv->kav/dot_general | solution.py:18
  494.0 12.1 %copy.20 = f32[170,128,128]{2,1,0:T(8,128)} copy(f32[170,128,128]{1,2,0:T(8,128)} %fusion.14) | data formatting | bytes 22282240 | tf_op jit(solution)/shard_map/kab,kbv->kav/dot_general | solution.py:18
  506.1 10.3 %pad.8 = f32[176,128,128]{2,1,0:T(8,128)} pad(f32[170,128,128]{2,1,0:T(8,128)} %copy.20, f32[]{:T(128)} %constant.31.clone.2), padding=0_6x0_0x0_0 | pad | bytes 22675460
  516.4 18.4 %copy.40 = f32[22,8,128,128]{3,1,2,0:T(8,128)} copy(f32[22,8,128,128]{3,2,1,0:T(8,128)} %bitcast.118) | data formatting | bytes 23068672
  534.8 7.3 fusion.30
  542.0 1.5 reshape.122
  543.7 1.9 copy.37
  545.6 5.3 gather_fusion.3
  550.9 23.4 %fusion.17 = f32[170,128,128]{1,2,0:T(8,128)} fusion(f32[170,128,128]{2,1,0:T(8,128)} %gather_fusion.3, f32[1,1,170,128,128]{4,3,2,1,0:T(8,128)} %param.6), kind=kOutput, calls=%fused_computation.15 | convolution fusion | flops 4278190080 | bytes 33423360 | tf_op jit(solution)/shard_map/kba,kbv->kav/dot_general | solution.py:20
  574.3 12.0 %copy.23 = f32[170,128,128]{2,1,0:T(8,128)} copy(f32[170,128,128]{1,2,0:T(8,128)} %fusion.17) | data formatting | bytes 22282240 | tf_op jit(solution)/shard_map/kba,kbv->kav/dot_general | solution.py:20
  586.3 10.4 %pad.9 = f32[176,128,128]{2,1,0:T(8,128)} pad(f32[170,128,128]{2,1,0:T(8,128)} %copy.23, f32[]{:T(128)} %constant.31.clone.2), padding=0_6x0_0x0_0 | pad | bytes 22675460
  596.7 18.3 %copy.41 = f32[22,8,128,128]{3,1,2,0:T(8,128)} copy(f32[22,8,128,128]{3,2,1,0:T(8,128)} %bitcast.113) | data formatting | bytes 23068672
  615.0 6.8 fusion.32
  623.1 1.4 fusion.41
  624.4 39.4 %reduce-scatter.11.cloned.1.call-done = f32[256,128]{1,0:T(8,128)} async-done(((f32[2048,128]{1,0:T(8,128)}), f32[256,128]{1,0:T(8,128)}) %reduce-scatter.11.cloned.1.call-update) | async-done | bytes 131088 | tf_op jit(solution)/shard_map/reduce_scatter | solution.py:56
  663.8 2.0 convolution_add_fusion
  665.8 144.7 %all-reduce.5.cloned.1.call-done = f32[128,128]{0,1:T(8,128)} async-done(((f32[128,128]{0,1:T(8,128)}), f32[128,128]{0,1:T(8,128)}) %all-reduce.5.cloned.1.call-update) | async-done | bytes 65552 | tf_op jit(solution)/shard_map/psum | solution.py:63
  812.4 11.7 %cholesky.55 = f32[128,128]{1,0:T(8,128)S(1)} custom-call(f32[128,128]{1,0:T(8,128)S(1)} %fusion.24), custom_call_target="Cholesky" | custom-call | tf_op jit(solution)/shard_map/jit(cholesky)/cholesky | solution.py:64
  825.4 9.8 %custom-call.10 = f32[1,128,128]{1,2,0:T(8,128)S(1)} custom-call(f32[1,128,128]{2,1,0:T(8,128)S(1)} %fusion.21), custom_call_target="InvertDiagBlocksLowerTriangular" | custom-call | tf_op jit(solution)/shard_map/triangular_solve/custom-call.0 | solution.py:37
  835.2 1.2 convolution_bitcast_fusion.1
  836.5 1.2 convolution_bitcast_fusion
  (43 shorter events, 11.1 us)
Async XLA Ops:
  6.5 41.7 %all-gather.11.cloned.1.call-start = ((), (), s32[]{:S(2)}) async-start(), calls=%async_computation.12 | async-start | bytes 1179648 | tf_op jit(solution)/shard_map/all_gather | solution.py:52
  8.2 124.6 %all-gather.13.cloned.1.call-start = ((), (), s32[]{:S(2)}) async-start(), calls=%async_computation.13 | async-start | bytes 2228224 | tf_op jit(solution)/shard_map/all_gather | solution.py:53
  9.0 208.3 %reduce-scatter.5.cloned.1.call-start = ((), (), s32[]{:S(2)}) async-start(), calls=%async_computation.4 | async-start | bytes 2228224 | tf_op jit(solution)/shard_map/reduce_scatter | solution.py:55
  132.7 125.2 %reduce-scatter.7.cloned.1.call-start = ((), (), s32[]{:S(2)}) async-start(), calls=%async_computation.5 | async-start | bytes 1179648 | tf_op jit(solution)/shard_map/reduce_scatter | solution.py:56
  217.2 186.8 %all-reduce.3.cloned.1.call-start = ((), (), s32[]{:S(2)}) async-start(), calls=%async_computation.6 | async-start | bytes 131072 | tf_op jit(solution)/shard_map/psum | solution.py:63
  260.0 203.6 %all-gather.7.cloned.1.call-start = ((), (), s32[]{:S(2)}) async-start(), calls=%async_computation.7 | async-start | bytes 1179648 | tf_op jit(solution)/shard_map/all_gather | solution.py:52
  430.6 113.1 %all-gather.9.cloned.1.call-start = ((), (), s32[]{:S(2)}) async-start(), calls=%async_computation.9 | async-start | bytes 2228224 | tf_op jit(solution)/shard_map/all_gather | solution.py:53
  432.5 190.5 %reduce-scatter.9.cloned.1.call-start = ((), (), s32[]{:S(2)}) async-start(), calls=%async_computation.8 | async-start | bytes 2228224 | tf_op jit(solution)/shard_map/reduce_scatter | solution.py:55
  543.6 120.2 %reduce-scatter.11.cloned.1.call-start = ((), (), s32[]{:S(2)}) async-start(), calls=%async_computation.10 | async-start | bytes 1179648 | tf_op jit(solution)/shard_map/reduce_scatter | solution.py:56
  623.0 187.6 %all-reduce.5.cloned.1.call-start = ((), (), s32[]{:S(2)}) async-start(), calls=%async_computation.11 | async-start | bytes 131072 | tf_op jit(solution)/shard_map/psum | solution.py:63
Sparse Core Ops, SparseCore 0:
  9.0 39.1 all-gather.10
  50.6 52.7 all-gather.12
  132.9 73.0 reduce-scatter.4
  217.4 40.5 reduce-scatter.6
  262.5 141.4 all-reduce.2
  430.7 32.8 all-gather.6
  466.1 53.9 all-gather.8
  543.7 73.1 reduce-scatter.8
  623.1 40.6 reduce-scatter.10
  669.1 141.4 all-reduce.4
where the time goes:
time: 855 us; the launch traced here: 846 us
  waiting for transfers between devices  437 us (51%)
  local copies, waits for them, and re-layouts  210 us (25%)
  matrix products  135 us (16%)
  other arithmetic  49.9 us (6%)
  between operations  14 us (2%)
    psum x2, waiting for transfers between devices, local(): gram_sum = lax.psum(partial_gram, ('row', 'col')) / total_rows  289 us
    unnamed x8, local copies, waits for them, and re-layouts  115 us
    reduce_scatter x2, waiting for transfers between devices, local(): lax.psum_scatter(out_cols, 'row', scatter_dimension=0, tiled=True)  78.7 us
    all_gather x2, waiting for transfers between devices, local(): col_side = lax.all_gather(current[1], 'row', axis=0, tiled=True)  68.6 us
    dot_general x2, matrix products, tile_products(): jnp.einsum('kab,kbv->kav', values, col_pieces, precision=exact_mode)  46.9 us
    dot_general x2, matrix products, tile_products(): jnp.einsum('kba,kbv->kav', values, row_pieces, precision=exact_mode)  46.8 us
    another operation x6, other arithmetic, local(): factor = jnp.linalg.cholesky(gram_sum)  24.8 us
    dot_general x2, local copies, waits for them, and re-layouts, tile_products(): jnp.einsum('kab,kbv->kav', values, col_pieces, precision=exact_mode)  24.3 us
  transfers between devices with their start and end apart: 10, of which 6 were waited for; matrix products, arithmetic and copies ran while one was open for 40% of the time, Pallas kernels for 0%

commit v1 on v0

--- a/solution.py
+++ b/solution.py
@@ -60,7 +60,7 @@
         partial_gram = partial_gram + jnp.einsum(
             "nv,nw->vw", factor_lower, factor_lower, precision=exact_mode
         )
-        gram_sum = lax.psum(partial_gram, ("row", "col")) / total_rows
+        gram_sum = jnp.sum(lax.all_gather(partial_gram, ("row", "col")), axis=0) / total_rows
         factor = jnp.linalg.cholesky(gram_sum)
         current = (normal_basis(applied[0], factor), normal_basis(applied[1], factor))
     upper, lower = current

time: 855 us -> 985 us (1.15)
  waiting for transfers between devices: 437 us -> 563 us
    all_gather x0 -> x2, waiting for transfers between devices: none -> 413 us  [local(): lax.all_gather(partial_gram, ('row', 'col'))]
    psum x2 -> x0, waiting for transfers between devices: 289 us -> none  [local(): gram_sum = lax.psum(partial_gram, ('row', 'col')) / total_rows]
  transfers between devices with their start and end apart: 10 -> 10, of which waited for: 6 -> 6; matrix products, arithmetic and copies ran while one was open for 40% -> 34% of each run, Pallas kernels for 0% -> 0%
where the time goes in v1:
time: 985 us; the launch traced here: 976 us
  waiting for transfers between devices  563 us (57%)
  local copies, waits for them, and re-layouts  210 us (21%)
  matrix products  135 us (14%)
  other arithmetic  54.2 us (6%)
  between operations  14 us (1%)
    all_gather x2, waiting for transfers between devices, local(): lax.all_gather(partial_gram, ('row', 'col'))  413 us
    unnamed x8, local copies, waits for them, and re-layouts  115 us
    reduce_scatter x2, waiting for transfers between devices, local(): lax.psum_scatter(out_cols, 'row', scatter_dimension=0, tiled=True)  78.6 us
    all_gather x2, waiting for transfers between devices, local(): col_side = lax.all_gather(current[1], 'row', axis=0, tiled=True)  70.5 us
    dot_general x2, matrix products, tile_products(): jnp.einsum('kab,kbv->kav', values, col_pieces, precision=exact_mode)  46.9 us
    dot_general x2, matrix products, tile_products(): jnp.einsum('kba,kbv->kav', values, row_pieces, precision=exact_mode)  46.8 us
    another operation x6, other arithmetic, local(): factor = jnp.linalg.cholesky(gram_sum)  24.8 us
    dot_general x2, local copies, waits for them, and re-layouts, tile_products(): jnp.einsum('kab,kbv->kav', values, col_pieces, precision=exact_mode)  24.3 us
  transfers between devices with their start and end apart: 10, of which 6 were waited for; matrix products, arithmetic and copies ran while one was open for 34% of the time, Pallas kernels for 0%

profile of v1, /device:TPU:1, one launch (start us, length us, event | category | flops | bytes accessed | tf_op | source)
XLA Modules:
  0.0 976.4 jit_solution(17352829358996605935)
XLA Ops:
  6.5 1.7 fusion.38
  10.6 37.6 %all-gather.15.cloned.1.call-done = f32[1,2048,128]{2,1,0:T(8,128)} async-done(((f32[1,256,128]{2,1,0:T(8,128)}), f32[1,2048,128]{2,1,0:T(8,128)}) %all-gather.15.cloned.1.call-update) | async-done | bytes 1048592 | tf_op jit(solution)/shard_map/all_gather | solution.py:52
  48.2 11.6 %gather_fusion = f32[170,128,128]{2,1,0:T(8,128)} fusion(f32[16,128,128]{2,1,0:T(8,128)} %bitcast.110, s32[1024]{0:T(1024)S(1)} %pad_clamp_fusion.1), kind=kCustom, calls=%fused_computation | custom fusion | bytes 22282920 | tf_op jit(solution)/shard_map/gather | solution.py:17
  59.8 23.3 %fusion.8 = f32[170,128,128]{1,2,0:T(8,128)} fusion(f32[170,128,128]{2,1,0:T(8,128)} %gather_fusion, f32[1,1,170,128,128]{4,3,2,1,0:T(8,128)} %param.6), kind=kOutput, calls=%fused_computation.12 | convolution fusion | flops 4278190080 | bytes 33423360 | tf_op jit(solution)/shard_map/kab,kbv->kav/dot_general | solution.py:18
  83.1 12.3 %copy.21 = f32[170,128,128]{2,1,0:T(8,128)} copy(f32[170,128,128]{1,2,0:T(8,128)} %fusion.8) | data formatting | bytes 22282240 | tf_op jit(solution)/shard_map/kab,kbv->kav/dot_general | solution.py:18
  95.3 10.5 %pad.6 = f32[176,128,128]{2,1,0:T(8,128)} pad(f32[170,128,128]{2,1,0:T(8,128)} %copy.21, f32[]{:T(128)} %constant.39.clone.1), padding=0_6x0_0x0_0 | pad | bytes 22675460
  105.8 18.3 %copy.41 = f32[22,8,128,128]{3,1,2,0:T(8,128)} copy(f32[22,8,128,128]{3,2,1,0:T(8,128)} %bitcast.116) | data formatting | bytes 23068672
  124.1 7.0 fusion.31
  131.2 1.5 reshape.116
  132.8 12.0 %gather_fusion.1 = f32[170,128,128]{2,1,0:T(8,128)} fusion(f32[32,128,128]{2,1,0:T(8,128)} %bitcast.112, s32[1024]{0:T(1024)S(1)} %pad_clamp_fusion), kind=kCustom, calls=%fused_computation.1 | custom fusion | bytes 22282920 | tf_op jit(solution)/shard_map/gather | solution.py:19
  144.8 23.4 %fusion.11 = f32[170,128,128]{1,2,0:T(8,128)} fusion(f32[170,128,128]{2,1,0:T(8,128)} %gather_fusion.1, f32[1,1,170,128,128]{4,3,2,1,0:T(8,128)} %param.6), kind=kOutput, calls=%fused_computation.13 | convolution fusion | flops 4278190080 | bytes 33423360 | tf_op jit(solution)/shard_map/kba,kbv->kav/dot_general | solution.py:20
  168.2 12.0 %copy.23 = f32[170,128,128]{2,1,0:T(8,128)} copy(f32[170,128,128]{1,2,0:T(8,128)} %fusion.11) | data formatting | bytes 22282240 | tf_op jit(solution)/shard_map/kba,kbv->kav/dot_general | solution.py:20
  180.3 10.4 %pad.7 = f32[176,128,128]{2,1,0:T(8,128)} pad(f32[170,128,128]{2,1,0:T(8,128)} %copy.23, f32[]{:T(128)} %constant.39.clone.1), padding=0_6x0_0x0_0 | pad | bytes 22675460
  190.7 18.4 %copy.42 = f32[22,8,128,128]{3,1,2,0:T(8,128)} copy(f32[22,8,128,128]{3,2,1,0:T(8,128)} %bitcast.118) | data formatting | bytes 23068672
  209.1 7.0 fusion.33
  217.3 1.4 fusion.40
  218.7 39.3 %reduce-scatter.7.cloned.1.call-done = f32[256,128]{1,0:T(8,128)} async-done(((f32[2048,128]{1,0:T(8,128)}), f32[256,128]{1,0:T(8,128)}) %reduce-scatter.7.cloned.1.call-update) | async-done | bytes 131088 | tf_op jit(solution)/shard_map/reduce_scatter | solution.py:56
  258.0 2.0 convolution_add_fusion.1
  260.0 206.6 %all-gather.19.cloned.1.call-done = f32[16384,128]{1,0:T(8,128)} async-done(((f32[128,128]{1,0:T(8,128)}), f32[16384,128]{1,0:T(8,128)}) %all-gather.19.cloned.1.call-update) | async-done | bytes 8388624 | tf_op jit(solution)/shard_map/all_gather | solution.py:63
  466.6 3.8 reduce_sum.18
  470.6 11.7 %cholesky.44 = f32[128,128]{1,0:T(8,128)S(1)} custom-call(f32[128,128]{1,0:T(8,128)S(1)} %fusion.27), custom_call_target="Cholesky" | custom-call | tf_op jit(solution)/shard_map/jit(cholesky)/cholesky | solution.py:64
  483.7 9.8 %custom-call.8 = f32[1,128,128]{1,2,0:T(8,128)S(1)} custom-call(f32[1,128,128]{2,1,0:T(8,128)S(1)} %fusion.20), custom_call_target="InvertDiagBlocksLowerTriangular" | custom-call | tf_op jit(solution)/shard_map/triangular_solve/custom-call.0 | solution.py:37
  493.5 1.9 convolution_bitcast_fusion.3
  495.4 1.9 convolution_bitcast_fusion.2
  497.4 32.9 %all-gather.11.cloned.1.call-done = f32[2048,128]{0,1:T(8,128)} async-done(((f32[256,128]{0,1:T(8,128)}), f32[2048,128]{0,1:T(8,128)}) %all-gather.11.cloned.1.call-update) | async-done | bytes 1048592 | tf_op jit(solution)/shard_map/all_gather | solution.py:52
  530.3 1.5 copy.39
  531.8 5.3 gather_fusion.2
  537.2 23.5 %fusion.14 = f32[170,128,128]{1,2,0:T(8,128)} fusion(f32[170,128,128]{2,1,0:T(8,128)} %gather_fusion.2, f32[1,1,170,128,128]{4,3,2,1,0:T(8,128)} %param.6), kind=kOutput, calls=%fused_computation.14 | convolution fusion | flops 4278190080 | bytes 33423360 | tf_op jit(solution)/shard_map/kab,kbv->kav/dot_general | solution.py:18
  560.7 12.0 %copy.28 = f32[170,128,128]{2,1,0:T(8,128)} copy(f32[170,128,128]{1,2,0:T(8,128)} %fusion.14) | data formatting | bytes 22282240 | tf_op jit(solution)/shard_map/kab,kbv->kav/dot_general | solution.py:18
  572.8 10.3 %pad.8 = f32[176,128,128]{2,1,0:T(8,128)} pad(f32[170,128,128]{2,1,0:T(8,128)} %copy.28, f32[]{:T(128)} %constant.39.clone.1), padding=0_6x0_0x0_0 | pad | bytes 22675460
  583.1 18.4 %copy.43 = f32[22,8,128,128]{3,1,2,0:T(8,128)} copy(f32[22,8,128,128]{3,2,1,0:T(8,128)} %bitcast.119) | data formatting | bytes 23068672
  601.5 7.3 fusion.30
  608.7 1.5 reshape.122
  610.4 1.9 copy.40
  612.3 5.3 gather_fusion.3
  617.6 23.4 %fusion.17 = f32[170,128,128]{1,2,0:T(8,128)} fusion(f32[170,128,128]{2,1,0:T(8,128)} %gather_fusion.3, f32[1,1,170,128,128]{4,3,2,1,0:T(8,128)} %param.6), kind=kOutput, calls=%fused_computation.15 | convolution fusion | flops 4278190080 | bytes 33423360 | tf_op jit(solution)/shard_map/kba,kbv->kav/dot_general | solution.py:20
  641.0 12.0 %copy.31 = f32[170,128,128]{2,1,0:T(8,128)} copy(f32[170,128,128]{1,2,0:T(8,128)} %fusion.17) | data formatting | bytes 22282240 | tf_op jit(solution)/shard_map/kba,kbv->kav/dot_general | solution.py:20
  653.0 10.4 %pad.9 = f32[176,128,128]{2,1,0:T(8,128)} pad(f32[170,128,128]{2,1,0:T(8,128)} %copy.31, f32[]{:T(128)} %constant.39.clone.1), padding=0_6x0_0x0_0 | pad | bytes 22675460
  663.4 18.3 %copy.44 = f32[22,8,128,128]{3,1,2,0:T(8,128)} copy(f32[22,8,128,128]{3,2,1,0:T(8,128)} %bitcast.120) | data formatting | bytes 23068672
  681.7 6.8 fusion.32
  689.8 1.4 fusion.41
  691.1 39.3 %reduce-scatter.11.cloned.1.call-done = f32[256,128]{1,0:T(8,128)} async-done(((f32[2048,128]{1,0:T(8,128)}), f32[256,128]{1,0:T(8,128)}) %reduce-scatter.11.cloned.1.call-update) | async-done | bytes 131088 | tf_op jit(solution)/shard_map/reduce_scatter | solution.py:56
  730.4 2.0 convolution_add_fusion
  732.5 206.7 %all-gather.21.cloned.1.call-done = f32[16384,128]{1,0:T(8,128)} async-done(((f32[128,128]{1,0:T(8,128)}), f32[16384,128]{1,0:T(8,128)}) %all-gather.21.cloned.1.call-update) | async-done | bytes 8388624 | tf_op jit(solution)/shard_map/all_gather | solution.py:63
  939.1 3.8 reduce_sum.19
  943.2 11.7 %cholesky.55 = f32[128,128]{1,0:T(8,128)S(1)} custom-call(f32[128,128]{1,0:T(8,128)S(1)} %fusion.24), custom_call_target="Cholesky" | custom-call | tf_op jit(solution)/shard_map/jit(cholesky)/cholesky | solution.py:64
  956.2 9.8 %custom-call.10 = f32[1,128,128]{1,2,0:T(8,128)S(1)} custom-call(f32[1,128,128]{2,1,0:T(8,128)S(1)} %fusion.21), custom_call_target="InvertDiagBlocksLowerTriangular" | custom-call | tf_op jit(solution)/shard_map/triangular_solve/custom-call.0 | solution.py:37
  966.0 1.2 convolution_bitcast_fusion.1
  (47 shorter events, 10.2 us)
Async XLA Ops:
  6.5 41.7 %all-gather.15.cloned.1.call-start = ((), (), s32[]{:S(2)}) async-start(), calls=%async_computation.10 | async-start | bytes 1179648 | tf_op jit(solution)/shard_map/all_gather | solution.py:52
  8.2 124.6 %all-gather.17.cloned.1.call-start = ((), (), s32[]{:S(2)}) async-start(), calls=%async_computation.11 | async-start | bytes 2228224 | tf_op jit(solution)/shard_map/all_gather | solution.py:53
  9.0 208.3 %reduce-scatter.5.cloned.1.call-start = ((), (), s32[]{:S(2)}) async-start(), calls=%async_computation.4 | async-start | bytes 2228224 | tf_op jit(solution)/shard_map/reduce_scatter | solution.py:55
  132.7 125.2 %reduce-scatter.7.cloned.1.call-start = ((), (), s32[]{:S(2)}) async-start(), calls=%async_computation.5 | async-start | bytes 1179648 | tf_op jit(solution)/shard_map/reduce_scatter | solution.py:56
  217.2 249.4 %all-gather.19.cloned.1.call-start = ((), (), s32[]{:S(2)}) async-start(), calls=%async_computation.12 | async-start | bytes 8454144 | tf_op jit(solution)/shard_map/all_gather | solution.py:63
  260.0 270.3 %all-gather.11.cloned.1.call-start = ((), (), s32[]{:S(2)}) async-start(), calls=%async_computation.6 | async-start | bytes 1179648 | tf_op jit(solution)/shard_map/all_gather | solution.py:52
  495.4 115.0 %all-gather.13.cloned.1.call-start = ((), (), s32[]{:S(2)}) async-start(), calls=%async_computation.8 | async-start | bytes 2228224 | tf_op jit(solution)/shard_map/all_gather | solution.py:53
  497.3 192.4 %reduce-scatter.9.cloned.1.call-start = ((), (), s32[]{:S(2)}) async-start(), calls=%async_computation.7 | async-start | bytes 2228224 | tf_op jit(solution)/shard_map/reduce_scatter | solution.py:55
  610.3 120.2 %reduce-scatter.11.cloned.1.call-start = ((), (), s32[]{:S(2)}) async-start(), calls=%async_computation.9 | async-start | bytes 1179648 | tf_op jit(solution)/shard_map/reduce_scatter | solution.py:56
  689.7 249.4 %all-gather.21.cloned.1.call-start = ((), (), s32[]{:S(2)}) async-start(), calls=%async_computation.13 | async-start | bytes 8454144 | tf_op jit(solution)/shard_map/all_gather | solution.py:63
Sparse Core Ops, SparseCore 0:
  9.0 39.1 all-gather.14
  50.6 52.7 all-gather.16
  132.9 73.0 reduce-scatter.4
  217.4 40.5 reduce-scatter.6
  260.1 206.4 all-gather.18
  495.5 34.7 all-gather.10
  532.5 53.9 all-gather.12
  610.4 73.1 reduce-scatter.8
  689.8 40.5 reduce-scatter.10
  732.6 206.4 all-gather.20
